TPU v7x, 512 devices: a whole 4x4x16 slice. The times are simulated.
512 devices in a mesh: mom: 32 (over z, core), hist: 16 (over y, x).
Axes of the slice: x: 4, y: 4, z: 16, core: 2. Of those that a mesh axis runs over, the one named last changes fastest.
Arguments:
- green_hist: float32 [2, 2, 2, 4096, 4096], P(None, None, None, 'mom', 'hist'), may hold values from 0.5 to 1.5
- sigma_row: float32 [2, 2, 2, 4096], P(None, None, None, 'hist'), may hold values from -6 to 6
- coupling_row: float32 [2, 2, 2, 4096], P(None, None, None, 'hist'), may hold values from -3 to 3
- prop_prev: float32 [2, 2, 2, 4096], P(None, None, None, 'mom'), may hold values from 0.5 to 1.5
- init_state: float32 [4], replicated, may hold values from 0.5 to 1.5
- state_rates: float32 [4], replicated, may hold values from 0.05 to 2
- source_row: float32 [4, 4096], P(None, 'hist'), may hold values from -6 to 6
- mom_ids: int32 [4096], P('mom'), may hold values from 0 to 4095, each once
- t_step: int32 [1], replicated, may hold values from 0 to 2999
- block_len: int32 [16], replicated, may hold values from 1 to 256, 2560 in all
Outputs:
- prop_new: float32 [2, 2, 2, 4096], P(None, None, None, 'mom')
- pp_row: float32 [4, 4096], P(None, 'hist')
- hyb_row: float32 [2, 2, 2, 4096], P(None, None, None, 'hist')
Inputs may be any that keep to these rules, and one draw needn't show every extreme that they name: `mom_ids`: each momentum point 0 .. 4095 appears once. `block_len`: the entries sum to 2560; the largest is 256.
All inputs are finite; a program needn't handle non-finite values.
Results may differ from a plain program's by a relative error of at most 0.00035.
Values sent between devices are 32-bit elements; how exact they have to be, the bound alone decides.
A program may use at most 64 MiB of HBM per device.

v0:
```python
import math
import jax
import jax.numpy as jnp
import numpy as np
from jax import lax
from jax.sharding import PartitionSpec as P

LK = 64
TIME_STEP = 0.005
HOPPING_TIME = 0.5
FIELD_STEP = 0.0025


def entering(value, axis, join, neutral):
    count, mine = (lax.axis_size(axis), lax.axis_index(axis))
    pieces = jax.tree.map(lambda part: lax.all_gather(part, axis), value)
    so_far = jax.tree.map(
        lambda part, zero: jnp.full_like(part, 0) + jnp.asarray(zero, part.dtype), value, neutral
    )

    def step(position, so_far):
        longer = join(so_far, jax.tree.map(lambda part: part[position], pieces))
        return jax.tree.map(lambda new, old: jnp.where(position < mine, new, old), longer, so_far)

    return lax.fori_loop(0, count - 1, step, so_far)


def from_root(value, axis, source):
    kept = jnp.where(lax.axis_index(axis) == source, value, 0).astype(value.dtype)
    return lax.psum(kept, axis)


def parity_sign(value):
    sign_value = 1
    for position in range(4):
        if value >> position & 1:
            sign_value = -sign_value
    return sign_value


def fock_table():
    table = np.zeros((2, 2, 4, 4), np.float32)
    for state_in in range(4):
        for orb_b in range(2):
            if state_in >> orb_b & 1:
                sign_b = parity_sign(state_in & (1 << orb_b) - 1)
                middle = state_in ^ 1 << orb_b
                for orb_a in range(2):
                    if not middle >> orb_a & 1:
                        sign_a = parity_sign(middle & (1 << orb_a) - 1)
                        state_out = middle | 1 << orb_a
                        table[orb_a, orb_b, state_out, state_in] += sign_a * sign_b
    return jnp.asarray(table, jnp.float32)


def complex_product(left, right):
    hp = lax.Precision.HIGHEST
    real_part = jnp.einsum("ab...,bc...->ac...", left[0], right[0], precision=hp) - jnp.einsum(
        "ab...,bc...->ac...", left[1], right[1], precision=hp
    )
    imag_part = jnp.einsum("ab...,bc...->ac...", left[0], right[1], precision=hp) + jnp.einsum(
        "ab...,bc...->ac...", left[1], right[0], precision=hp
    )
    return jnp.stack([real_part, imag_part])


def memory_sum(weighted, history):
    hp = lax.Precision.HIGHEST
    real_part = jnp.einsum("abs,bcks->ack", weighted[0], history[0], precision=hp) - jnp.einsum(
        "abs,bcks->ack", weighted[1], history[1], precision=hp
    )
    imag_part = jnp.einsum("abs,bcks->ack", weighted[0], history[1], precision=hp) + jnp.einsum(
        "abs,bcks->ack", weighted[1], history[0], precision=hp
    )
    return jnp.stack([real_part, imag_part])


def row_product(current, history):
    hp = lax.Precision.HIGHEST
    real_part = jnp.einsum("ack,bcks->abs", current[0], history[0], precision=hp) + jnp.einsum(
        "ack,bcks->abs", current[1], history[1], precision=hp
    )
    imag_part = jnp.einsum("ack,bcks->abs", current[1], history[0], precision=hp) - jnp.einsum(
        "ack,bcks->abs", current[0], history[1], precision=hp
    )
    return jnp.stack([real_part, imag_part])


def momentum_phase(mom_ids, t_step, total):
    field = FIELD_STEP * t_step[0].astype(jnp.float32)
    along_x = 2.0 * math.pi * (mom_ids % LK).astype(jnp.float32) / LK
    along_y = 2.0 * math.pi * (mom_ids // LK).astype(jnp.float32) / (total // LK)
    energy = -2.0 * (jnp.cos(along_x - field) + jnp.cos(along_y - field))
    angle = HOPPING_TIME * energy
    return (jnp.cos(angle), jnp.sin(angle))


def advance(previous, memory, cosine, sine):
    summed = previous + memory
    real_part = cosine * summed[0] + sine * summed[1]
    imag_part = cosine * summed[1] - sine * summed[0]
    return jnp.stack([real_part, imag_part])


def compose(earlier, later):
    hp = lax.Precision.HIGHEST
    mats = jnp.einsum("...nm,...mk->...nk", later[0], earlier[0], precision=hp)
    vecs = jnp.einsum("...nm,...m->...n", later[0], earlier[1], precision=hp) + later[1]
    return (mats, vecs)


def on_device(
    green_hist,
    sigma_row,
    coupling_row,
    prop_prev,
    init_state,
    state_rates,
    source_row,
    mom_ids,
    t_step,
    block_len,
):
    slots_dev = green_hist.shape[-1]
    mom_dev = green_hist.shape[3]
    mom_count = lax.axis_size("mom")
    hist_count = lax.axis_size("hist")
    total = mom_dev * mom_count
    hist_pos = lax.axis_index("hist")
    length = lax.dynamic_slice_in_dim(block_len, hist_pos, 1, 0)[0]
    live_mask = jnp.arange(slots_dev, dtype=jnp.int32) < length
    weight = jnp.where(live_mask, jnp.float32(TIME_STEP), jnp.float32(0.0))
    memory_part = memory_sum(sigma_row * weight, green_hist)
    cosine, sine = momentum_phase(mom_ids, t_step, total)
    memory = lax.psum(memory_part, "hist")
    prop_new = advance(prop_prev, memory, cosine, sine)
    row_part = row_product(prop_new, green_hist) / total
    row_part = jnp.where(live_mask, row_part, jnp.float32(0.0))
    local_row = lax.psum(row_part, "mom")
    delta = complex_product(local_row, coupling_row)
    table = fock_table()
    lam = jnp.einsum("abs,abnm->snm", delta[0], table, precision=lax.Precision.HIGHEST)
    retain = jnp.diag(jnp.exp(-state_rates / (slots_dev * hist_count)))
    identity = jnp.eye(init_state.shape[0], dtype=jnp.float32)
    mats = jnp.where(live_mask[:, None, None], retain[None] - TIME_STEP * lam, identity[None])
    vecs = jnp.where(live_mask[:, None], TIME_STEP * source_row.T, jnp.float32(0.0))
    cum_mats, cum_vecs = lax.associative_scan(compose, (mats, vecs), axis=0)
    block_map = (cum_mats[-1], cum_vecs[-1])
    prior = entering(block_map, "hist", compose, (identity, jnp.zeros_like(init_state)))
    start_state = jnp.dot(prior[0], init_state, precision=lax.Precision.HIGHEST) + prior[1]
    states = (
        jnp.einsum("snm,m->sn", cum_mats, start_state, precision=lax.Precision.HIGHEST) + cum_vecs
    )
    final_state = from_root(states[-1], "hist", hist_count - 1)
    pp_row = states.T
    scale = 1.0 / jnp.sqrt(1.0 + jnp.sum(final_state * final_state))
    hyb_row = delta * scale
    return (prop_new, pp_row, hyb_row)


def solution(mesh):
    placed = (
        P(None, None, None, "mom", "hist"),
        P(None, None, None, "hist"),
        P(None, None, None, "hist"),
        P(None, None, None, "mom"),
        P(),
        P(),
        P(None, "hist"),
        P("mom"),
        P(),
        P(),
    )
    return jax.shard_map(
        on_device,
        mesh=mesh,
        in_specs=placed,
        out_specs=(P(None, None, None, "mom"), P(None, "hist"), P(None, None, None, "hist")),
        check_vma=False,
    )
```

profile of v0, /device:TPU:2, one launch (start us, length us, event | category | flops | bytes accessed | tf_op | source)
XLA Modules:
  0.0 226.2 jit_solution(4658161577168113196)
XLA Ops:
  1.3 0.6 copy-done.15
  2.0 0.6 dynamic_slice.17
  2.5 0.6 iota_compare_fusion.1
  3.2 0.7 broadcast_select_fusion.2
  3.9 0.6 copy-done.14
  4.8 0.6 copy-done.13
  5.4 0.2 slice.367
  5.6 0.2 slice.333
  5.8 0.2 slice.332
  6.1 0.7 copy-done.11
  7.1 1.3 fusion.111
  8.4 0.5 convolution_bitcast_fusion.8
  8.9 0.5 fusion.22
  9.5 0.5 convolution_bitcast_fusion.6
  10.0 0.5 fusion.21
  10.6 41.4 %psum.21 = f32[2,2,2,128]{3,1,2,0:T(2,128)S(1)} all-reduce(f32[2,2,2,128]{3,1,2,0:T(2,128)S(1)} %pad_maximum_fusion.6), channel_id=1, replica_groups=mesh['mom'=32,'hist'=16] {'hist'}, use_global_device_ids=true, to_apply=%region_0.1 | all-reduce | flops 1024 | bytes 8192 | tf_op jit(solution)/shard_map/psum | solution.py:135
  52.0 0.4 convolution_bitcast_fusion.2
  52.3 0.4 fusion.18
  52.7 0.6 copy.173
  53.3 0.4 convolution_bitcast_fusion.4
  53.6 0.4 fusion.16
  54.0 48.5 %psum.22 = f32[2,2,2,256]{3,1,2,0:T(2,128)S(1)} all-reduce(f32[2,2,2,256]{3,1,2,0:T(2,128)S(1)} %fusion.70), channel_id=1, replica_groups=mesh['mom'=32,'hist'=16] {'mom'}, use_global_device_ids=true, to_apply=%region_1.2 | all-reduce | flops 2048 | bytes 16384 | tf_op jit(solution)/shard_map/psum | solution.py:139
  102.9 1.8 fusion.28
  104.7 1.8 fusion.32
  106.5 1.9 convolution_subtract_fusion
  108.4 1.9 fusion.11
  110.6 0.6 copy-done.17
  111.2 0.2 fusion.14
  111.4 0.4 slice.295
  112.3 0.4 slice.294
  112.6 0.4 slice.296
  113.6 1.0 fusion.113
  115.3 0.6 fusion.38
  116.5 0.4 fusion.46
  117.4 0.3 fusion.54
  120.0 0.4 convolution_add_fusion.1
  120.8 0.7 slice-done.5
  122.3 0.7 slice-done.4
  123.9 0.6 slice-done.3
  125.3 0.2 fusion.56
  125.6 0.6 slice-done.2
  126.9 0.2 pad.106
  127.1 0.2 pad.107
  127.3 0.3 fusion.48
  127.7 0.6 slice-done.1
  129.0 0.7 slice-done.6
  129.7 0.2 pad.128
  130.0 0.2 pad.129
  130.4 21.8 %all-gather = f32[16,1,4]{2,1,0:T(1,128)S(1)} all-gather(f32[1,1,4]{2,1,0:T(1,128)S(1)} %bitcast.255), channel_id=1, replica_groups=mesh['mom'=32,'hist'=16] {'hist'}, dimensions={0}, use_global_device_ids=true | all-gather | bytes 272 | tf_op jit(solution)/shard_map/all_gather | solution.py:16
  152.1 0.4 pad.108
  152.5 0.4 pad.109
  152.9 0.6 fusion.40
  153.6 0.6 slice-done
  154.2 0.8 pad.110
  155.1 0.8 pad.111
  156.1 1.0 fusion.34
  157.2 1.7 pad.112
  158.9 1.7 pad.113
  160.5 21.1 %all_gather.6 = f32[16,4,4]{2,1,0:T(4,128)S(1)} all-gather(f32[1,4,4]{2,1,0:T(4,128)S(1)} %slice_add_fusion), channel_id=1, replica_groups=mesh['mom'=32,'hist'=16] {'hist'}, dimensions={0}, use_global_device_ids=true | all-gather | bytes 1088 | tf_op jit(solution)/shard_map/all_gather | solution.py:16
  181.7 4.4 %while.16 = (s32[]{:T(128)}, f32[4,4]{1,0:T(4,128)S(1)}, f32[4]{0:T(128)S(1)}, s32[]{:T(128)}, f32[16,4,4]{2,1,0:T(4,128)S(1)}, /*index=5*/f32[16,4]{1,0:T(8,128)S(1)}, s32[]{:T(128)}, s32[]{:T(128)}) while((s32[]{:T(128)}, f32[4,4]{1,0:T(4,128)S(1)}, f32[4]{0:T(128)S(1)}, s32[]{:T(128)}, f32[16,4,4]{2,1,0:T(4,128)S(1)}, ...), condition=%wide.region_3.4_spmd.clone, body=%wide.region_2.3_spmd.clone.sunk | while | flops 996 | bytes 12644 | solution.py:25
  186.2 0.4 multiply_reduce_fusion
  186.9 37.5 %psum.23 = f32[4]{0:T(128)S(1)} all-reduce(f32[4]{0:T(128)S(1)} %fusion.86), channel_id=1, replica_groups=mesh['mom'=32,'hist'=16] {'hist'}, use_global_device_ids=true, to_apply=%region_4.5 | all-reduce | flops 4 | bytes 32 | tf_op jit(solution)/shard_map/psum | solution.py:30
  224.3 0.6 multiply_reduce_fusion.14
  225.6 0.6 maximum_multiply_fusion.1
  (253 shorter events, 16.2 us)
Async XLA Ops:
  0.6 185.4 %copy-start = (f32[4]{0:T(128)S(1)}, f32[4]{0:T(128)}, u32[]{:S(2)}) copy-start(f32[4]{0:T(128)} %param.17) | copy-start | bytes 52
  1.3 0.7 copy-start.15
  3.2 0.7 copy-start.16
  3.9 0.7 copy-start.14
  4.7 0.7 copy-start.13
  5.4 0.7 copy-start.8
  5.4 0.7 copy-start.10
  6.1 0.7 copy-start.11
  8.4 43.5 %copy-start.1 = (f32[2,2,2,128,256]{4,3,2,1,0:T(8,128)S(1)}, f32[2,2,2,128,256]{4,3,2,1,0:T(8,128)}, u32[]{:S(2)}) copy-start(f32[2,2,2,128,256]{4,3,2,1,0:T(8,128)} %param.13) | copy-start | bytes 3145732
  10.5 41.4 %copy-start.12 = (f32[2,2,2,128]{3,2,1,0:T(2,128)S(1)}, f32[2,2,2,128]{3,2,1,0:T(2,128)}, u32[]{:S(2)}) copy-start(f32[2,2,2,128]{3,2,1,0:T(2,128)} %param.16) | copy-start | bytes 12292
  110.5 0.7 copy-start.17
  114.5 38.4 %copy-start.2 = (f32[128,4,4]{2,1,0:T(4,128)}, f32[128,4,4]{2,1,0:T(4,128)S(1)}, u32[]{:S(2)}) copy-start(f32[128,4,4]{2,1,0:T(4,128)S(1)} %fusion.113) | copy-start | bytes 24580
  115.8 11.5 %copy-start.3 = (f32[64,4,4]{2,1,0:T(4,128)}, f32[64,4,4]{2,1,0:T(4,128)S(1)}, u32[]{:S(2)}) copy-start(f32[64,4,4]{2,1,0:T(4,128)S(1)} %fusion.38) | copy-start | bytes 12292
  116.8 8.5 %copy-start.4 = (f32[32,4,4]{2,1,0:T(4,128)}, f32[32,4,4]{2,1,0:T(4,128)S(1)}, u32[]{:S(2)}) copy-start(f32[32,4,4]{2,1,0:T(4,128)S(1)} %fusion.46) | copy-start | bytes 6148
  117.7 6.0 %copy-start.5 = (f32[16,4,4]{2,1,0:T(4,128)}, f32[16,4,4]{2,1,0:T(4,128)S(1)}, u32[]{:S(2)}) copy-start(f32[16,4,4]{2,1,0:T(4,128)S(1)} %fusion.54) | copy-start | bytes 3076
  118.4 3.7 %copy-start.6 = (f32[8,4,4]{2,1,0:T(4,128)}, f32[8,4,4]{2,1,0:T(4,128)S(1)}, u32[]{:S(2)}) copy-start(f32[8,4,4]{2,1,0:T(4,128)S(1)} %fusion.62) | copy-start | bytes 1540
  119.1 1.5 copy-start.7
  120.7 0.7 slice-start.5
  122.3 0.7 slice-start.4
  123.8 0.7 slice-start.3
  125.6 0.7 slice-start.2
  127.7 0.7 slice-start.1
  129.0 0.7 slice-start.6
  153.5 0.7 slice-start
  186.7 38.9 %copy-start.9 = (f32[256,4]{0,1:T(4,128)}, f32[256,4]{0,1:T(4,128)S(1)}, u32[]{:S(2)}) copy-start(f32[256,4]{0,1:T(4,128)S(1)} %add_add_fusion) | copy-start | bytes 12292
where the time goes:
time: 227 us; the launch traced here: 226 us
  blocking collectives  170 us (75%)
  local copies, waits for them, and re-layouts  26.3 us (12%)
  matrix products  21.2 us (9%)
  other arithmetic  5.78 us (3%)
  between operations  2.72 us (1%)
    psum x1, blocking collectives, on_device(): local_row = lax.psum(row_part, 'mom')  48.5 us
    all_gather x2, blocking collectives, entering(): pieces = jax.tree.map(lambda part: lax.all_gather(part, axis), value)  42.9 us
    psum x1, blocking collectives, on_device(): memory = lax.psum(memory_part, 'hist')  41.4 us
    psum x1, blocking collectives, from_root(): return lax.psum(kept, axis)  37.5 us
    slice x45, local copies, waits for them, and re-layouts, on_device(): cum_mats, cum_vecs = lax.associative_scan(compose, (mats, vecs), axis=0)  9.1 us
    pad x28, local copies, waits for them, and re-layouts, on_device(): cum_mats, cum_vecs = lax.associative_scan(compose, (mats, vecs), axis=0)  8.22 us
    dot_general x30, matrix products, compose(): mats = jnp.einsum('...nm,...mk->...nk', later[0], earlier[0], precision=hp)  7.39 us
    unnamed x50, local copies, waits for them, and re-layouts  5.18 us

commit v1 on v0

--- a/solution.py
+++ b/solution.py
@@ -136,7 +136,8 @@
     prop_new = advance(prop_prev, memory, cosine, sine)
     row_part = row_product(prop_new, green_hist) / total
     row_part = jnp.where(live_mask, row_part, jnp.float32(0.0))
-    local_row = lax.psum(row_part, "mom")
+    terms = lax.all_gather(row_part, "mom")
+    local_row = jnp.sum(terms, axis=0)
     delta = complex_product(local_row, coupling_row)
     table = fock_table()
     lam = jnp.einsum("abs,abnm->snm", delta[0], table, precision=lax.Precision.HIGHEST)

time: 227 us -> 211 us (0.930)
  the two profiles are of different devices: /device:TPU:2 before, /device:TPU:32 now
where the time goes in v1:
time: 211 us; the launch traced here: 210 us
  blocking collectives  154 us (73%)
  local copies, waits for them, and re-layouts  26.4 us (13%)
  matrix products  20.9 us (10%)
  other arithmetic  5.94 us (3%)
  between operations  2.72 us (1%)
    psum x1, blocking collectives, on_device(): memory = lax.psum(memory_part, 'hist')  40.7 us
    all_gather x2, blocking collectives, entering(): pieces = jax.tree.map(lambda part: lax.all_gather(part, axis), value)  40.4 us
    psum x1, blocking collectives, from_root(): return lax.psum(kept, axis)  38.1 us
    all_gather x1, blocking collectives, on_device(): terms = lax.all_gather(row_part, 'mom')  35 us
    slice x45, local copies, waits for them, and re-layouts, on_device(): cum_mats, cum_vecs = lax.associative_scan(compose, (mats, vecs), axis=0)  9.24 us
    pad x28, local copies, waits for them, and re-layouts, on_device(): cum_mats, cum_vecs = lax.associative_scan(compose, (mats, vecs), axis=0)  8.22 us
    dot_general x30, matrix products, compose(): mats = jnp.einsum('...nm,...mk->...nk', later[0], earlier[0], precision=hp)  7.39 us
    unnamed x52, local copies, waits for them, and re-layouts  5.54 us

profile of v1, /device:TPU:32, one launch (start us, length us, event | category | flops | bytes accessed | tf_op | source)
XLA Modules:
  0.0 210.3 jit_solution(7038498421506635376)
XLA Ops:
  1.3 0.6 copy-done.15
  2.0 0.6 dynamic_slice.17
  2.5 0.6 iota_compare_fusion.1
  3.2 0.7 broadcast_select_fusion.2
  3.9 0.6 copy-done.14
  4.8 0.6 copy-done.13
  5.4 0.2 slice.367
  5.6 0.2 slice.333
  5.8 0.2 slice.332
  6.1 0.7 copy-done.11
  7.1 1.3 fusion.115
  8.4 0.5 convolution_bitcast_fusion.8
  8.9 0.5 fusion.22
  9.5 0.5 convolution_bitcast_fusion.6
  10.0 0.5 fusion.21
  10.6 40.7 %psum.14 = f32[2,2,2,128]{3,1,2,0:T(2,128)S(1)} all-reduce(f32[2,2,2,128]{3,1,2,0:T(2,128)S(1)} %pad_maximum_fusion.6), channel_id=1, replica_groups=mesh['mom'=32,'hist'=16] {'hist'}, use_global_device_ids=true, to_apply=%region_0.1 | all-reduce | flops 1024 | bytes 8192 | tf_op jit(solution)/shard_map/psum | solution.py:135
  51.3 0.4 convolution_bitcast_fusion.2
  51.6 0.4 fusion.18
  52.0 0.6 copy.169
  52.6 0.4 convolution_bitcast_fusion.4
  53.0 0.4 fusion.16
  53.4 35.0 %all_gather.10 = f32[32,2,2,2,256]{4,3,2,1,0:T(2,128)S(1)} all-gather(f32[1,2,2,2,256]{4,3,2,1,0:T(2,128)S(1)} %copy.152), channel_id=1, replica_groups=mesh['mom'=32,'hist'=16] {'mom'}, dimensions={0}, use_global_device_ids=true | all-gather | bytes 270336 | tf_op jit(solution)/shard_map/all_gather | solution.py:139
  88.8 1.8 fusion.28
  90.7 1.8 fusion.34
  92.5 1.9 convolution_subtract_fusion
  94.3 1.9 fusion.11
  96.6 0.6 copy-done.17
  97.2 0.2 fusion.14
  97.4 0.4 slice.295
  98.3 0.4 slice.294
  98.6 0.4 slice.296
  99.5 1.0 fusion.118
  101.2 0.6 fusion.42
  102.4 0.4 fusion.50
  103.4 0.3 fusion.58
  104.0 0.2 slice.347
  106.7 0.7 slice-done.5
  108.2 0.7 slice-done.4
  109.8 0.6 slice-done.3
  111.2 0.2 fusion.60
  111.5 0.6 slice-done.2
  112.8 0.2 pad.106
  113.0 0.2 pad.107
  113.2 0.3 fusion.52
  113.6 0.6 slice-done.1
  114.9 0.7 slice-done.6
  115.6 0.2 pad.128
  115.9 0.2 pad.129
  116.3 17.0 %all-gather = f32[16,1,4]{2,1,0:T(1,128)S(1)} all-gather(f32[1,1,4]{2,1,0:T(1,128)S(1)} %bitcast.257), channel_id=1, replica_groups=mesh['mom'=32,'hist'=16] {'hist'}, dimensions={0}, use_global_device_ids=true | all-gather | bytes 272 | tf_op jit(solution)/shard_map/all_gather | solution.py:16
  133.2 0.4 pad.108
  133.7 0.4 pad.109
  134.1 0.6 fusion.44
  134.7 0.6 slice-done
  135.4 0.8 pad.110
  136.2 0.8 pad.111
  137.2 1.0 fusion.38
  138.4 1.7 pad.112
  140.0 1.7 pad.113
  141.7 23.4 %all_gather.11 = f32[16,4,4]{2,1,0:T(4,128)S(1)} all-gather(f32[1,4,4]{2,1,0:T(4,128)S(1)} %slice_add_fusion), channel_id=1, replica_groups=mesh['mom'=32,'hist'=16] {'hist'}, dimensions={0}, use_global_device_ids=true | all-gather | bytes 1088 | tf_op jit(solution)/shard_map/all_gather | solution.py:16
  165.1 4.4 %while.16 = (s32[]{:T(128)}, f32[4,4]{1,0:T(4,128)S(1)}, f32[4]{0:T(128)S(1)}, s32[]{:T(128)}, f32[16,4,4]{2,1,0:T(4,128)S(1)}, /*index=5*/f32[16,4]{1,0:T(8,128)S(1)}, s32[]{:T(128)}, s32[]{:T(128)}) while((s32[]{:T(128)}, f32[4,4]{1,0:T(4,128)S(1)}, f32[4]{0:T(128)S(1)}, s32[]{:T(128)}, f32[16,4,4]{2,1,0:T(4,128)S(1)}, ...), condition=%wide.region_3.4_spmd.clone, body=%wide.region_2.3_spmd.clone.sunk | while | flops 996 | bytes 12644 | solution.py:25
  169.6 0.4 multiply_reduce_fusion
  170.3 38.1 %psum.15 = f32[4]{0:T(128)S(1)} all-reduce(f32[4]{0:T(128)S(1)} %fusion.90), channel_id=1, replica_groups=mesh['mom'=32,'hist'=16] {'hist'}, use_global_device_ids=true, to_apply=%region_4.5 | all-reduce | flops 4 | bytes 32 | tf_op jit(solution)/shard_map/psum | solution.py:30
  208.4 0.6 multiply_reduce_fusion.14
  209.7 0.6 maximum_multiply_fusion.1
  (255 shorter events, 16.3 us)
Async XLA Ops:
  0.6 168.8 %copy-start = (f32[4]{0:T(128)S(1)}, f32[4]{0:T(128)}, u32[]{:S(2)}) copy-start(f32[4]{0:T(128)} %param.17) | copy-start | bytes 52
  1.3 0.7 copy-start.15
  3.2 0.7 copy-start.16
  3.9 0.7 copy-start.14
  4.7 0.7 copy-start.13
  5.4 0.7 copy-start.8
  5.4 0.7 copy-start.10
  6.1 0.7 copy-start.11
  8.4 42.8 %copy-start.1 = (f32[2,2,2,128,256]{4,3,2,1,0:T(8,128)S(1)}, f32[2,2,2,128,256]{4,3,2,1,0:T(8,128)}, u32[]{:S(2)}) copy-start(f32[2,2,2,128,256]{4,3,2,1,0:T(8,128)} %param.13) | copy-start | bytes 3145732
  10.5 40.7 %copy-start.12 = (f32[2,2,2,128]{3,2,1,0:T(2,128)S(1)}, f32[2,2,2,128]{3,2,1,0:T(2,128)}, u32[]{:S(2)}) copy-start(f32[2,2,2,128]{3,2,1,0:T(2,128)} %param.16) | copy-start | bytes 12292
  96.4 0.7 copy-start.17
  100.5 33.6 %copy-start.2 = (f32[128,4,4]{2,1,0:T(4,128)}, f32[128,4,4]{2,1,0:T(4,128)S(1)}, u32[]{:S(2)}) copy-start(f32[128,4,4]{2,1,0:T(4,128)S(1)} %fusion.118) | copy-start | bytes 24580
  101.8 11.4 %copy-start.3 = (f32[64,4,4]{2,1,0:T(4,128)}, f32[64,4,4]{2,1,0:T(4,128)S(1)}, u32[]{:S(2)}) copy-start(f32[64,4,4]{2,1,0:T(4,128)S(1)} %fusion.42) | copy-start | bytes 12292
  102.8 8.4 %copy-start.4 = (f32[32,4,4]{2,1,0:T(4,128)}, f32[32,4,4]{2,1,0:T(4,128)S(1)}, u32[]{:S(2)}) copy-start(f32[32,4,4]{2,1,0:T(4,128)S(1)} %fusion.50) | copy-start | bytes 6148
  103.6 5.9 %copy-start.5 = (f32[16,4,4]{2,1,0:T(4,128)}, f32[16,4,4]{2,1,0:T(4,128)S(1)}, u32[]{:S(2)}) copy-start(f32[16,4,4]{2,1,0:T(4,128)S(1)} %fusion.58) | copy-start | bytes 3076
  104.5 3.5 %copy-start.6 = (f32[8,4,4]{2,1,0:T(4,128)}, f32[8,4,4]{2,1,0:T(4,128)S(1)}, u32[]{:S(2)}) copy-start(f32[8,4,4]{2,1,0:T(4,128)S(1)} %fusion.66) | copy-start | bytes 1540
  105.2 1.3 copy-start.7
  106.6 0.7 slice-start.5
  108.2 0.7 slice-start.4
  109.7 0.7 slice-start.3
  111.5 0.7 slice-start.2
  113.6 0.7 slice-start.1
  114.9 0.7 slice-start.6
  134.6 0.7 slice-start
  170.1 39.6 %copy-start.9 = (f32[256,4]{0,1:T(4,128)}, f32[256,4]{0,1:T(4,128)S(1)}, u32[]{:S(2)}) copy-start(f32[256,4]{0,1:T(4,128)S(1)} %add_add_fusion) | copy-start | bytes 12292
